TPU v7x, 32 devices: a whole 2x2x4 slice. The times are simulated.
32 devices in a mesh: gx: 8 (over y, x, core), gy: 4 (over z).
Axes of the slice: x: 2, y: 2, z: 4, core: 2. Of those that a mesh axis runs over, the one named last changes fastest.
Arguments:
- slip_field: float32 [256, 3, 128], P(('gy', 'gx')), may hold values from -6 to 6
- positions: float32 [256, 3, 128], P(('gy', 'gx')), may hold values from -6 to 6
- neighbours: int32 [256, 8], P(('gy', 'gx')), may hold values from 0 to 63, as said below
- near_counts: int32 [256], P(('gy', 'gx')), may hold values from 1 to 8, as said below
- cluster_basis: float32 [256, 16, 3, 128], P(('gy', 'gx')), may hold values from -0.4375 to 0.4375
- transfer: float32 [62, 16, 16], replicated, may hold values from -1 to 1
- coupling: float32 [62, 16, 16], replicated, may hold values from -1.5 to 1.5
- prestress: float32 [256, 3, 128], P(('gy', 'gx')), may hold values from -6 to 6
- normal_stress: float32 [256, 128], P(('gy', 'gx')), may hold values from 1 to 3
- friction: float32 [256, 128], P(('gy', 'gx')), may hold values from 0.3 to 0.9
- compliance: float32 [256, 128], P(('gy', 'gx')), may hold values from 0.1 to 1
- slip_state: int32 [256, 128], P(('gy', 'gx')), may hold values 0 or 1
- cell_index: int32 [256, 4, 128], P(('gy', 'gx')), may hold values from 0 to 8191, as said below
- cell_weight: float32 [256, 4, 128], P(('gy', 'gx')), may hold values from 0.1 to 0.5
- dilation: float32 [256, 128], P(('gy', 'gx')), may hold values from 1 to 10
- pressure: float32 [64, 512], P('gx', 'gy'), may hold values from -4 to 4
- mobility: float32 [64, 512], P('gx', 'gy'), may hold values from 0.05 to 0.24
Outputs:
- final_slip: float32 [256, 3, 128], P(('gy', 'gx'))
- final_pressure: float32 [64, 512], P('gx', 'gy')
Inputs may be any that keep to these rules, and one draw needn't show every extreme that they name: `neighbours`: entry 0 of a row is the cluster's own number within its subtree; the entries of a row are distinct and lie within 8 clusters of the cluster's own number, counted cyclically within its subtree of 64 clusters. Only the first near_counts[c] entries of a row of neighbours are used; some cluster has exactly 8. `slip_state`: 1 marks an element that slips. `cell_index`: the four cells of an element are band rows r and r + 1 (counted cyclically over the 64 rows) at columns b and b + 1 of the band, in that order: (r, b), (r + 1, b), (r, b + 1), (r + 1, b + 1). For an element of cluster c with j = (c % 64) // 8, both rows lie in (j - 1) * 8 to (j + 2) * 8 - 1, cyclically; both ends are reached in every draw.
All inputs are finite; a program needn't handle non-finite values. No bound on the sum of `slip_state` on one device may be relied on, other than what follows from the above.
Results may differ from a plain program's by a relative error of at most 0.00027.
Values sent between devices are 32-bit elements; how exact they have to be, the bound alone decides.
A program may use at most 64 MiB of HBM per device.

v0:
```python
import functools

import jax
import jax.numpy as jnp
from jax import lax
from jax.experimental import pallas as pl
from jax.experimental.pallas import tpu as pltpu
from jax.sharding import PartitionSpec as P

ITERS = 2
FLOW_STEPS = 2
HIGHEST = lax.Precision.HIGHEST
KERNEL_SCALE = 0.04
SOFTENING = 0.25
MESH = pl.DeviceIdType.MESH
AROUND = ((-1, 0), (1, 0), (0, -1), (0, 1), (-1, -1), (-1, 1), (1, -1), (1, 1))
NT = (((1,), (1,)), ((), ()))


def kernel(
    nx, ny, levels,
    nbr_ref, count_ref, slip_ref, pos_ref, basis_ref, transfer_ref, coupling_ref,
    prestress_ref, normal_ref, friction_ref, compliance_ref, state_ref,
    cell_ref, weight_ref, dilation_ref, pressure_ref, mobility_ref,
    out_slip, out_pressure,
    path_t, path_c, pos_halo, slip_halo, slip_now, pos_b, slip_b, near_acc, far_s,
    moment_out, moment_in, row_w, col_hot, at_s, dil_s,
    p_now, p_halo, src_out, src_in, flow_in, mob_in,
    local_sem, send_sem, recv_sem, msend_sem, mrecv_sem,
):
    gx = lax.axis_index("gx")
    gy = lax.axis_index("gy")
    flat = gy * nx + gx
    devices = nx * ny
    comps, clusters, csize = slip_ref.shape
    slots = nbr_ref.shape[1]
    rank = basis_ref.shape[2]
    frows, fcols = pressure_ref.shape
    width = moment_out.shape[-1]
    subtree = clusters * nx
    strips = csize // 8

    barrier = pltpu.get_barrier_semaphore()

    def greet(step, carry):
        other = lax.rem(flat + step, devices)
        pl.semaphore_signal(
            barrier, inc=1,
            device_id={"gx": lax.rem(other, nx), "gy": lax.div(other, nx)},
            device_id_type=MESH,
        )
        return carry

    lax.fori_loop(1, devices, greet, 0)

    local = []
    for level in range(levels):
        node = 2 * devices - 2 * (devices >> level) + lax.div(flat, 1 << level)
        local.append(pltpu.make_async_copy(transfer_ref.at[node], path_t.at[level], local_sem.at[level]))
        local.append(pltpu.make_async_copy(coupling_ref.at[node], path_c.at[level], local_sem.at[levels + level]))
    for copy in local:
        copy.start()

    def remote(src, dst, number, dgx, dgy):
        return pltpu.make_async_remote_copy(
            src_ref=src, dst_ref=dst,
            send_sem=send_sem.at[number], recv_sem=recv_sem.at[number],
            device_id={"gx": lax.rem(gx + dgx + nx, nx), "gy": lax.rem(gy + dgy + ny, ny)},
            device_id_type=MESH,
        )

    started = []

    def send(src, dst, number, dgx, dgy):
        copy = remote(src, dst, number, dgx, dgy)
        copy.start()
        started.append(copy)
        return copy

    def send_both(src_back, src_ahead, dst, number):
        ahead = send(src_ahead, dst.at[0], number, 1, 0)
        back = send(src_back, dst.at[1], number + 1, -1, 0)
        return [ahead, back]

    def wait_in(copies):
        for copy in copies:
            copy.wait_recv()

    def spread(table, ref, base):
        def body(i, carry):
            columns = jnp.transpose(ref[i])
            for c in range(clusters):
                table[base + c, i] = jnp.broadcast_to(columns[:, c : c + 1], (csize, csize))
            return carry
        lax.fori_loop(0, comps, body, 0)

    def spread_own(table, ref):
        spread(table, ref, clusters)

    def spread_halo(table, ref):
        spread(table, ref.at[0], 0)
        spread(table, ref.at[1], 2 * clusters)

    def near(first, last):
        def one_cluster(c, carry):
            targets = [jnp.broadcast_to(pos_ref[i, pl.ds(c, 1), :], (8, csize)) for i in range(comps)]

            def one_slot(k, sums):
                number = nbr_ref[c, k]
                place = lax.rem(number - gx * clusters + clusters + subtree, subtree)
                place = jnp.minimum(place, 3 * clusters - 1)
                slipping = jnp.where(k < count_ref[c], place, 3 * clusters)
                sums = list(sums)
                for strip in range(strips):
                    rows = pl.ds(strip * 8, 8)
                    r = [targets[i] - pos_b[place, i, rows, :] for i in range(comps)]
                    s = [slip_b[slipping, i, rows, :] for i in range(comps)]
                    q = (r[0] * r[0] + r[1] * r[1]) + (r[2] * r[2] + SOFTENING)
                    inverse = lax.rsqrt(q)
                    along = (r[0] * s[0] + r[1] * s[1]) + r[2] * s[2]
                    scaled = along * (inverse * inverse)
                    for i in range(comps):
                        sums[i] = sums[i] + inverse * (s[i] + r[i] * scaled)
                return tuple(sums)

            if first == 0:
                start = tuple(jnp.zeros((8, csize), jnp.float32) for _ in range(comps))
            else:
                start = tuple(near_acc[i, c] for i in range(comps))
            sums = lax.fori_loop(first, last, one_slot, start)
            for i in range(comps):
                near_acc[i, c] = sums[i]
            return carry

        lax.fori_loop(0, clusters, one_cluster, 0)

    def moment_row(ref, lift):
        total = jnp.zeros((rank, csize), jnp.float32)
        for c in range(clusters):
            for i in range(comps):
                total = total + basis_ref[c, i] * ref[i, c : c + 1, :]
        column = jnp.sum(total, axis=1, keepdims=True)
        return jnp.sum(column * lift, axis=0, keepdims=True)

    def send_moments(it, ref, lift):
        moment_out[it] = moment_row(ref, lift)
        moment_in[it, flat] = jnp.zeros((1, width), jnp.float32)

        def body(step, carry):
            other = lax.rem(flat + step, devices)
            pltpu.make_async_remote_copy(
                src_ref=moment_out.at[it], dst_ref=moment_in.at[it, flat],
                send_sem=msend_sem.at[it], recv_sem=mrecv_sem.at[it],
                device_id={"gx": lax.rem(other, nx), "gy": lax.div(other, nx)},
                device_id_type=MESH,
            ).start()
            return carry

        lax.fori_loop(1, devices, body, 0)

    def wait_moments(it, sem):
        block = moment_in.at[it, pl.ds(0, devices - 1)]
        pltpu.make_async_copy(block, block, sem.at[it]).wait()

    spread_own(pos_b, pos_ref)
    spread_own(slip_b, slip_ref)
    slip_b[3 * clusters] = jnp.zeros((comps, csize, csize), jnp.float32)

    lane_rows = lax.broadcasted_iota(jnp.int32, (3 * frows, csize), 0)
    col_rows = lax.broadcasted_iota(jnp.int32, (fcols, csize), 0)
    first_cell = cell_ref[:, 0, :]
    cell_row = lax.div(first_cell, fcols)
    cell_col = first_cell - cell_row * fcols
    band_rows = frows * nx
    rim_row = lax.rem(cell_row - gx * frows + frows + band_rows, band_rows)
    for c in range(clusters):
        here = lane_rows == rim_row[c : c + 1, :]
        below = lane_rows == rim_row[c : c + 1, :] + 1
        w = [weight_ref[c, k : k + 1, :] for k in range(4)]
        row_w[c, 0] = jnp.where(here, w[0], 0.0) + jnp.where(below, w[1], 0.0)
        row_w[c, 1] = jnp.where(here, w[2], 0.0) + jnp.where(below, w[3], 0.0)
        hot = jnp.where(col_rows == cell_col[c : c + 1, :], 1.0, 0.0)
        col_hot[c] = hot.astype(jnp.bfloat16)

    for copy in local:
        copy.wait()
    place_rows = lax.broadcasted_iota(jnp.int32, (rank, width), 0)
    place_lanes = lax.broadcasted_iota(jnp.int32, (rank, width), 1)
    dot = functools.partial(jnp.dot, precision=HIGHEST, preferred_element_type=jnp.float32)
    chain = jnp.where(
        lax.broadcasted_iota(jnp.int32, (rank, rank), 0) == lax.broadcasted_iota(jnp.int32, (rank, rank), 1),
        1.0, 0.0,
    )
    lift = jnp.zeros((rank, width), jnp.float32)
    across = jnp.zeros((rank, width), jnp.float32)
    for level in range(levels):
        put = jnp.where(place_lanes == place_rows + level * rank, 1.0, 0.0)
        lift = lift + dot(chain, put)
        across = across + dot(dot(chain, path_c[level]), put)
        if level + 1 < levels:
            chain = dot(chain, path_t[level])

    node_ids = lax.broadcasted_iota(jnp.int32, (devices, width), 0)
    lane_level = lax.div(lax.broadcasted_iota(jnp.int32, (devices, width), 1), rank)
    sibling_mask = jnp.zeros((devices, width), jnp.bool_)
    for level in range(levels):
        own = lax.div(flat, 1 << level)
        sibling = own + 1 - 2 * lax.rem(own, 2)
        sibling_mask = sibling_mask | ((lane_level == level) & (lax.shift_right_logical(node_ids, level) == sibling))

    pl.semaphore_wait(barrier, devices - 1)

    base = 0
    waits_slip = send_both(slip_ref, slip_ref, slip_halo.at[0], base)
    waits_pos = send_both(pos_ref, pos_ref, pos_halo, base + 2)
    send_moments(0, slip_ref, lift)
    waits_p = send_both(pressure_ref, pressure_ref, p_halo.at[0], base + 4)
    waits_mob = []
    for number, (dgx, dgy) in enumerate(AROUND[:4]):
        waits_mob.append(send(mobility_ref, mob_in.at[number], base + 6 + number, -dgx, -dgy))
    base = base + 10

    near(0, 1)
    wait_in(waits_slip)
    wait_in(waits_pos)
    spread_halo(slip_b, slip_halo.at[0])
    spread_halo(pos_b, pos_halo)
    near(1, slots)
    wait_in(waits_mob)

    lanes = lax.broadcasted_iota(jnp.int32, (3 * frows, fcols), 1)
    inside = []
    for dgx, dgy in AROUND:
        ok = jnp.bool_(True)
        if dgx:
            ok = ok & (gx + dgx >= 0) & (gx + dgx < nx)
        if dgy:
            ok = ok & (gy + dgy >= 0) & (gy + dgy < ny)
        inside.append(jnp.where(ok, 1.0, 0.0))
    blank = jnp.zeros((frows, fcols), jnp.float32)
    mob_mid = jnp.concatenate([mob_in[0] * inside[0], mobility_ref[...], mob_in[1] * inside[1]], axis=0)
    mob_left = jnp.concatenate([blank, mob_in[2] * inside[2], blank], axis=0)
    mob_right = jnp.concatenate([blank, mob_in[3] * inside[3], blank], axis=0)
    rows3 = 3 * frows

    def stencil(mid, before, behind, mobility):
        beside = pltpu.roll(mid, 1, 0) + pltpu.roll(mid, rows3 - 1, 0)
        left = jnp.where(lanes == 0, pltpu.roll(before, 1, 1), pltpu.roll(mid, 1, 1))
        right = jnp.where(lanes == fcols - 1, pltpu.roll(behind, fcols - 1, 1), pltpu.roll(mid, fcols - 1, 1))
        return mid + mobility * ((beside + (left + right)) - 4.0 * mid)

    pressure = pressure_ref[...]
    old_slip = slip_ref
    for it in range(ITERS):
        last = it == ITERS - 1
        wait_moments(it, mrecv_sem)
        gathered = moment_in[it].reshape(devices, width)
        siblings = jnp.sum(jnp.where(sibling_mask, gathered, 0.0), axis=0, keepdims=True)
        incoming = jnp.sum(across * siblings, axis=1, keepdims=True)
        for c in range(clusters):
            for i in range(comps):
                far_s[i, c : c + 1, :] = jnp.sum(basis_ref[c, i] * incoming, axis=0, keepdims=True)
        wait_in(waits_p)
        table = jnp.concatenate([p_halo[it, 0], pressure, p_halo[it, 1]], axis=0)
        for c in range(clusters):
            columns = jnp.broadcast_to(cell_col[c : c + 1, :], (rows3, csize))
            g0 = jnp.take_along_axis(table, columns, axis=1)
            g1 = jnp.take_along_axis(pltpu.roll(table, fcols - 1, 1), columns, axis=1)
            at_s[c : c + 1, :] = jnp.sum(row_w[c, 0] * g0 + row_w[c, 1] * g1, axis=0, keepdims=True)
        stress = []
        for i in range(comps):
            near_part = KERNEL_SCALE * jnp.sum(near_acc[i], axis=1)
            stress.append(prestress_ref[i] - (near_part + far_s[i]))
        square = (stress[0] * stress[0] + stress[1] * stress[1]) + stress[2] * stress[2]
        effective = normal_ref[...] - at_s[...]
        factor = jnp.maximum(1.0 - friction_ref[...] * effective / jnp.sqrt(square + 1.0), 0.0)
        scale = state_ref[...].astype(jnp.float32) * compliance_ref[...] * factor
        step = [scale * stress[i] for i in range(comps)]
        target = out_slip if last else slip_now
        for i in range(comps):
            target[i] = old_slip[i] + step[i]
        old_slip = target
        if not last:
            waits_slip = send_both(slip_now, slip_now, slip_halo.at[it + 1], base)
            base = base + 2
            send_moments(it + 1, slip_now, lift)
        dil_s[...] = dilation_ref[...] * ((step[0] * step[0] + step[1] * step[1]) + step[2] * step[2])
        loaded = jnp.zeros((4 * rows3, fcols), jnp.float32)
        for c in range(clusters):
            dilated = dil_s[c : c + 1, :]
            left = jnp.concatenate([row_w[c, 0] * dilated, row_w[c, 1] * dilated], axis=0)
            high = left.astype(jnp.bfloat16)
            low = (left - high.astype(jnp.float32)).astype(jnp.bfloat16)
            loaded = loaded + lax.dot_general(
                jnp.concatenate([high, low], axis=0), col_hot[c], NT,
                preferred_element_type=jnp.float32,
            )
        loaded = loaded[: 2 * rows3] + loaded[2 * rows3 :]
        loaded = loaded[:rows3] + pltpu.roll(loaded[rows3:], 1, 1)
        src_out[it, 0] = loaded[:frows]
        src_out[it, 1] = loaded[2 * frows :]
        waits_src = send_both(src_out.at[it, 0], src_out.at[it, 1], src_in.at[it], base)
        base = base + 2
        if not last:
            spread_own(slip_b, slip_now)
            near(0, 1)
        wait_in(waits_src)
        pressure = pressure + (loaded[frows : 2 * frows] + (src_in[it, 0] + src_in[it, 1]))
        p_now[2 * it] = pressure
        waits_flow = []
        for number, (dgx, dgy) in enumerate(AROUND):
            waits_flow.append(send(p_now.at[2 * it], flow_in.at[it, number], base, -dgx, -dgy))
            base = base + 1
        if not last:
            wait_in(waits_slip)
            spread_halo(slip_b, slip_halo.at[it + 1])
            near(1, slots // 2)
        wait_in(waits_flow)
        around = [flow_in[it, number] * inside[number] for number in range(8)]
        mid = jnp.concatenate([around[0], pressure, around[1]], axis=0)
        before = jnp.concatenate([around[4], around[2], around[6]], axis=0)
        behind = jnp.concatenate([around[5], around[3], around[7]], axis=0)
        mid1 = stencil(mid, before, behind, mob_mid)
        before1 = stencil(before, before, mid, mob_left)
        behind1 = stencil(behind, mid, behind, mob_right)
        pressure = stencil(mid1, before1, behind1, mob_mid)[frows : 2 * frows]
        if last:
            out_pressure[...] = pressure
        else:
            p_now[2 * it + 1] = pressure
            waits_p = send_both(p_now.at[2 * it + 1], p_now.at[2 * it + 1], p_halo.at[it + 1], base)
            base = base + 2
            near(slots // 2, slots)

    for copy in started:
        copy.wait_send()
    for it in range(ITERS):
        wait_moments(it, msend_sem)


def shards(
    slip_field, positions, neighbours, near_counts, cluster_basis, transfer, coupling,
    prestress, normal_stress, friction, compliance, slip_state, cell_index, cell_weight,
    dilation, pressure, mobility,
):
    nx = lax.axis_size("gx")
    ny = lax.axis_size("gy")
    devices = nx * ny
    levels = devices.bit_length() - 1
    slip_field, positions, prestress = (
        jnp.transpose(x, (1, 0, 2)) for x in (slip_field, positions, prestress)
    )
    cluster_basis = jnp.transpose(cluster_basis, (0, 2, 1, 3))
    comps, clusters, csize = slip_field.shape
    rank = transfer.shape[1]
    frows, fcols = pressure.shape
    width = (levels * rank + 127) // 128 * 128
    f32 = jnp.float32
    copies = 10 + ITERS * 14
    vmem = pl.BlockSpec(memory_space=pltpu.VMEM)
    smem = pl.BlockSpec(memory_space=pltpu.SMEM)
    hbm = pl.BlockSpec(memory_space=pl.ANY)
    new_slip, new_pressure = pl.pallas_call(
        functools.partial(kernel, nx, ny, levels),
        out_shape=(
            jax.ShapeDtypeStruct(slip_field.shape, f32),
            jax.ShapeDtypeStruct(pressure.shape, f32),
        ),
        in_specs=[smem, smem, vmem, vmem, vmem, hbm, hbm] + [vmem] * 10,
        out_specs=(vmem, vmem),
        scratch_shapes=[
            pltpu.VMEM((levels, rank, rank), f32),
            pltpu.VMEM((levels, rank, rank), f32),
            pltpu.VMEM((2,) + slip_field.shape, f32),
            pltpu.VMEM((ITERS, 2) + slip_field.shape, f32),
            pltpu.VMEM(slip_field.shape, f32),
            pltpu.VMEM((3 * clusters, comps, csize, csize), f32),
            pltpu.VMEM((3 * clusters + 1, comps, csize, csize), f32),
            pltpu.VMEM((comps, clusters, 8, csize), f32),
            pltpu.VMEM(slip_field.shape, f32),
            pltpu.VMEM((ITERS, 1, width), f32),
            pltpu.VMEM((ITERS, devices, 1, width), f32),
            pltpu.VMEM((clusters, 2, 3 * frows, csize), f32),
            pltpu.VMEM((clusters, fcols, csize), jnp.bfloat16),
            pltpu.VMEM((clusters, csize), f32),
            pltpu.VMEM((clusters, csize), f32),
            pltpu.VMEM((2 * ITERS, frows, fcols), f32),
            pltpu.VMEM((ITERS, 2, frows, fcols), f32),
            pltpu.VMEM((ITERS, 2, frows, fcols), f32),
            pltpu.VMEM((ITERS, 2, frows, fcols), f32),
            pltpu.VMEM((ITERS, 8, frows, fcols), f32),
            pltpu.VMEM((4, frows, fcols), f32),
            pltpu.SemaphoreType.DMA((2 * levels,)),
            pltpu.SemaphoreType.DMA((copies,)),
            pltpu.SemaphoreType.DMA((copies,)),
            pltpu.SemaphoreType.DMA((ITERS,)),
            pltpu.SemaphoreType.DMA((ITERS,)),
        ],
        compiler_params=pltpu.CompilerParams(collective_id=0, has_side_effects=True),
        name="coupling",
    )(
        neighbours, near_counts, slip_field, positions, cluster_basis, transfer, coupling,
        prestress, normal_stress, friction, compliance, slip_state,
        cell_index, cell_weight, dilation, pressure, mobility,
    )
    return jnp.transpose(new_slip, (1, 0, 2)), new_pressure


def solution(mesh):
    by_cluster = ("gy", "gx")
    in_specs = (
        P(by_cluster, None, None),
        P(by_cluster, None, None),
        P(by_cluster, None),
        P(by_cluster),
        P(by_cluster, None, None, None),
        P(),
        P(),
        P(by_cluster, None, None),
        P(by_cluster, None),
        P(by_cluster, None),
        P(by_cluster, None),
        P(by_cluster, None),
        P(by_cluster, None, None),
        P(by_cluster, None, None),
        P(by_cluster, None),
        P("gx", "gy"),
        P("gx", "gy"),
    )
    out_specs = (P(by_cluster, None, None), P("gx", "gy"))
    return jax.shard_map(shards, mesh=mesh, in_specs=in_specs, out_specs=out_specs, check_vma=False)
```

profile of v0, /device:TPU:0, one launch (start us, length us, event | category | flops | bytes accessed | tf_op | source)
XLA Modules:
  0.0 45.3 jit_solution(14074504092127793558)
XLA Ops:
  0.6 0.0 copy-start
  0.6 2.0 %copy.19.transfer_ref = f32[62,16,16]{2,1,0:T(8,128)} copy(f32[62,16,16]{0,2,1:T(8,128)} %param.22) | data formatting | bytes 126976 | tf_op args[5]
  2.6 0.0 copy-done
  2.6 1.1 %copy.20.coupling_ref = f32[62,16,16]{2,1,0:T(8,128)} copy(f32[62,16,16]{0,2,1:T(8,128)S(1)} %copy-done) | data formatting | bytes 126976 | tf_op args[6]
  3.7 39.7 %coupling.1 = (f32[3,8,128]{2,1,0:T(8,128)}, f32[8,128]{1,0:T(8,128)}) custom-call(s32[8,8]{1,0:T(8,128)} %nbr_ref.1, s32[8]{0:T(128)} %count_ref.1, f32[3,8,128]{2,1,0:T(8,128)} %bitcast.6, f32[3,8,128]{2,1,0:T(8,128)} %bitcast.7, f32[8,3,16,128]{3,2,1,0:T(8,128)} %bitcast.5, f32[62,16,16]{2,1,0:T(8,128)} %copy.19.transfer_ref, ...), custom_call_target="tpu_custom_call" | custom-call | tf_op jit(solution)/shard_map/coupling/pallas_call | solution.py:363
  43.4 0.0 copy-start.1
  43.4 1.3 %copy.23 = f32[8,3,128]{2,0,1:T(8,128)} copy(f32[8,3,128]{2,0,1:T(8,128)} %bitcast.9) | data formatting | bytes 24576
  44.7 0.0 copy-done.1
  44.7 0.6 %copy.24 = f32[8,128]{1,0:T(8,128)} copy(f32[8,128]{1,0:T(8,128)S(1)} %copy-done.1) | data formatting | bytes 8192
Async XLA Ops:
  0.6 2.0 %copy-start = (f32[62,16,16]{0,2,1:T(8,128)S(1)}, f32[62,16,16]{0,2,1:T(8,128)}, u32[]{:S(2)}) copy-start(f32[62,16,16]{0,2,1:T(8,128)} %param.23) | copy-start | bytes 190468
  43.4 1.3 %copy-start.1 = (f32[8,128]{1,0:T(8,128)S(1)}, f32[8,128]{1,0:T(8,128)}, u32[]{:S(2)}) copy-start(f32[8,128]{1,0:T(8,128)} %get-tuple-element.9) | copy-start | bytes 12292
where the time goes:
time: 45.5 us; the launch traced here: 45.3 us
  Pallas kernels  39.7 us (87%)
  local copies, waits for them, and re-layouts  4.95 us (11%)
  between operations  0.66 us (1%)
    pallas_call x1, Pallas kernels, shards(): pl.pallas_call(functools.partial(kernel, nx, ny, levels), out_shape=(jax....  39.7 us
    unnamed x8, local copies, waits for them, and re-layouts  4.95 us

commit v1 on v0

--- a/solution.py
+++ b/solution.py
@@ -23,10 +23,10 @@
     prestress_ref, normal_ref, friction_ref, compliance_ref, state_ref,
     cell_ref, weight_ref, dilation_ref, pressure_ref, mobility_ref,
     out_slip, out_pressure,
-    path_t, path_c, pos_halo, slip_halo, slip_now, pos_b, slip_b, near_acc, far_s,
+    pos_halo, slip_halo, slip_now, pos_b, slip_b, near_acc, far_s,
     moment_out, moment_in, row_w, col_hot, at_s, dil_s,
     p_now, p_halo, src_out, src_in, flow_in, mob_in,
-    local_sem, send_sem, recv_sem, msend_sem, mrecv_sem,
+    send_sem, recv_sem, msend_sem, mrecv_sem,
 ):
     gx = lax.axis_index("gx")
     gy = lax.axis_index("gy")
@@ -52,14 +52,6 @@
         return carry
 
     lax.fori_loop(1, devices, greet, 0)
-
-    local = []
-    for level in range(levels):
-        node = 2 * devices - 2 * (devices >> level) + lax.div(flat, 1 << level)
-        local.append(pltpu.make_async_copy(transfer_ref.at[node], path_t.at[level], local_sem.at[level]))
-        local.append(pltpu.make_async_copy(coupling_ref.at[node], path_c.at[level], local_sem.at[levels + level]))
-    for copy in local:
-        copy.start()
 
     def remote(src, dst, number, dgx, dgy):
         return pltpu.make_async_remote_copy(
@@ -182,11 +174,39 @@
         hot = jnp.where(col_rows == cell_col[c : c + 1, :], 1.0, 0.0)
         col_hot[c] = hot.astype(jnp.bfloat16)
 
-    for copy in local:
-        copy.wait()
     place_rows = lax.broadcasted_iota(jnp.int32, (rank, width), 0)
     place_lanes = lax.broadcasted_iota(jnp.int32, (rank, width), 1)
     dot = functools.partial(jnp.dot, precision=HIGHEST, preferred_element_type=jnp.float32)
+    level_rows = (levels + 7) // 8 * 8
+    nodes = transfer_ref.shape[2]
+    row_level = lax.broadcasted_iota(jnp.int32, (level_rows, nodes), 0)
+    node_lane = lax.broadcasted_iota(jnp.int32, (level_rows, nodes), 1)
+    pick = jnp.zeros((level_rows, nodes), jnp.float32)
+    for level in range(levels):
+        node = 2 * devices - 2 * (devices >> level) + lax.div(flat, 1 << level)
+        pick = pick + jnp.where((row_level == level) & (node_lane == node), 1.0, 0.0)
+    square_lanes = lax.broadcasted_iota(jnp.int32, (rank, rank * rank), 1)
+    square_rows = lax.broadcasted_iota(jnp.int32, (rank, rank * rank), 0)
+    keep = lax.div(square_lanes, rank) == square_rows
+    fold = jnp.where(
+        lax.rem(lax.broadcasted_iota(jnp.int32, (rank * rank, rank), 0), rank)
+        == lax.broadcasted_iota(jnp.int32, (rank * rank, rank), 1),
+        1.0, 0.0,
+    )
+
+    def path_of(ref):
+        flat_rows = lax.dot_general(
+            pick, ref[...].reshape(rank * rank, nodes), NT,
+            precision=HIGHEST, preferred_element_type=jnp.float32,
+        )
+        spread_rows = jnp.concatenate(
+            [jnp.where(keep, flat_rows[level : level + 1], 0.0) for level in range(levels)], axis=0
+        )
+        folded = dot(spread_rows, fold)
+        return [folded[level * rank : (level + 1) * rank] for level in range(levels)]
+
+    path_t = path_of(transfer_ref)
+    path_c = path_of(coupling_ref)
     chain = jnp.where(
         lax.broadcasted_iota(jnp.int32, (rank, rank), 0) == lax.broadcasted_iota(jnp.int32, (rank, rank), 1),
         1.0, 0.0,
@@ -353,24 +373,22 @@
     cluster_basis = jnp.transpose(cluster_basis, (0, 2, 1, 3))
     comps, clusters, csize = slip_field.shape
     rank = transfer.shape[1]
+    transfer, coupling = (jnp.transpose(x, (1, 2, 0)) for x in (transfer, coupling))
     frows, fcols = pressure.shape
     width = (levels * rank + 127) // 128 * 128
     f32 = jnp.float32
     copies = 10 + ITERS * 14
     vmem = pl.BlockSpec(memory_space=pltpu.VMEM)
     smem = pl.BlockSpec(memory_space=pltpu.SMEM)
-    hbm = pl.BlockSpec(memory_space=pl.ANY)
     new_slip, new_pressure = pl.pallas_call(
         functools.partial(kernel, nx, ny, levels),
         out_shape=(
             jax.ShapeDtypeStruct(slip_field.shape, f32),
             jax.ShapeDtypeStruct(pressure.shape, f32),
         ),
-        in_specs=[smem, smem, vmem, vmem, vmem, hbm, hbm] + [vmem] * 10,
+        in_specs=[smem, smem] + [vmem] * 15,
         out_specs=(vmem, vmem),
         scratch_shapes=[
-            pltpu.VMEM((levels, rank, rank), f32),
-            pltpu.VMEM((levels, rank, rank), f32),
             pltpu.VMEM((2,) + slip_field.shape, f32),
             pltpu.VMEM((ITERS, 2) + slip_field.shape, f32),
             pltpu.VMEM(slip_field.shape, f32),
@@ -390,7 +408,6 @@
             pltpu.VMEM((ITERS, 2, frows, fcols), f32),
             pltpu.VMEM((ITERS, 8, frows, fcols), f32),
             pltpu.VMEM((4, frows, fcols), f32),
-            pltpu.SemaphoreType.DMA((2 * levels,)),
             pltpu.SemaphoreType.DMA((copies,)),
             pltpu.SemaphoreType.DMA((copies,)),
             pltpu.SemaphoreType.DMA((ITERS,)),

time: 45.5 us -> 43.4 us (0.954)
  local copies, waits for them, and re-layouts: 4.95 us -> 1.9 us
  Pallas kernels: 39.7 us -> 40.7 us
    unnamed x8 -> x4, local copies, waits for them, and re-layouts: 4.95 us -> 1.9 us
    pallas_call x1, Pallas kernels: 39.7 us -> 40.7 us  [shards(): pl.pallas_call(functools.partial(kernel, nx, ny, levels), out_shape=(jax....]
where the time goes in v1:
time: 43.4 us; the launch traced here: 43.2 us
  Pallas kernels  40.7 us (94%)
  local copies, waits for them, and re-layouts  1.9 us (4%)
  between operations  0.65 us (1%)
    pallas_call x1, Pallas kernels, shards(): pl.pallas_call(functools.partial(kernel, nx, ny, levels), out_shape=(jax....  40.7 us
    unnamed x4, local copies, waits for them, and re-layouts  1.9 us

profile of v1, /device:TPU:0, one launch (start us, length us, event | category | flops | bytes accessed | tf_op | source)
XLA Modules:
  0.0 43.2 jit_solution(1527088319164456010)
XLA Ops:
  0.6 40.7 %coupling.1 = (f32[3,8,128]{2,1,0:T(8,128)}, f32[8,128]{1,0:T(8,128)}) custom-call(s32[8,8]{1,0:T(8,128)} %nbr_ref.1, s32[8]{0:T(128)} %count_ref.1, f32[3,8,128]{2,1,0:T(8,128)} %bitcast.11, f32[3,8,128]{2,1,0:T(8,128)} %bitcast.12, f32[8,3,16,128]{3,2,1,0:T(8,128)} %bitcast.7, f32[16,16,62]{2,1,0:T(8,128)} %bitcast.8, f32[16,16,62]{2,1,0:T(8,128)} %bitcast.9, ...), custom_call_target="tpu_custom_call" | custom-call | tf_op jit(solution)/shard_map/coupling/pallas_call | solution.py:383
  41.3 0.0 copy-start
  41.3 1.3 %copy.21 = f32[8,3,128]{2,0,1:T(8,128)} copy(f32[8,3,128]{2,0,1:T(8,128)} %bitcast.10) | data formatting | bytes 24576
  42.6 0.0 copy-done
  42.6 0.6 %copy.22 = f32[8,128]{1,0:T(8,128)} copy(f32[8,128]{1,0:T(8,128)S(1)} %copy-done) | data formatting | bytes 8192
Async XLA Ops:
  41.3 1.3 %copy-start = (f32[8,128]{1,0:T(8,128)S(1)}, f32[8,128]{1,0:T(8,128)}, u32[]{:S(2)}) copy-start(f32[8,128]{1,0:T(8,128)} %get-tuple-element.9) | copy-start | bytes 12292
